TPU v7x, 32 devices: a whole 2x2x4 slice. The times are simulated.
32 devices in a mesh: space: 8 (over y, x, core), chan: 4 (over z).
Axes of the slice: x: 2, y: 2, z: 4, core: 2. Of those that a mesh axis runs over, the one named last changes fastest.
Arguments:
- points: bfloat16 [256, 8, 16384], P('chan', 'space'), may hold values from -6 to 6
- point_cell: int32 [8, 16384], P('space'), may hold values from 0 to 4096, as said below
- conv_weight: bfloat16 [27, 256, 256], P(None, 'chan'), may hold values from -0.109375 to 0.109375
- conv_bias: bfloat16 [256], P('chan'), may hold values from -3 to 3
- neighbors: int32 [64, 27], P('space'), may hold values from -1 to 23, as said below
Outputs:
- voxel_out: bfloat16 [256, 32768], P('chan', 'space')
- point_out: bfloat16 [256, 8, 16384], P('chan', 'space')
Inputs may be any that keep to these rules, and one draw needn't show every extreme that they name: `point_cell`: in each aligned block of 2048 slots from one sender the live slots (cell below 4096) come first; in every draw some owner receives 2048 live slots from every sender. `neighbors`: entry 13 is the block's own slot 8 + b; blocks of one owner lie on a 4 x (4) grid of a strip, strips of owners d and d+1 adjacent.
All inputs are finite; a program needn't handle non-finite values.
Results may differ from a plain program's by a relative error of at most 0.01.
Values may be sent and summed in bfloat16 or wider, within the bound.
A program may use at most 128 MiB of HBM per device.

v0:
```python
import jax
import jax.numpy as jnp
import numpy as np
from jax import lax
from jax.sharding import PartitionSpec as P


def extended_2(cells, sides, width):
    for axis, dim in sides:
        count = lax.axis_size(axis)
        ends = count - 1
        head = lax.slice_in_dim(cells, 0, width, axis=dim)
        tail = lax.slice_in_dim(cells, cells.shape[dim] - width, cells.shape[dim], axis=dim)
        cells = jnp.concatenate(
            [
                lax.ppermute(tail, axis, [(i, (i + 1) % count) for i in range(ends)]),
                cells,
                lax.ppermute(head, axis, [((i + 1) % count, i) for i in range(ends)]),
            ],
            axis=dim,
        )
    return cells


def reach_tables(coord_x, coord_y, coord_z):

    def split_axis(values):
        moved = np.where(values < 0, -1, np.where(values > 7, 1, 0))
        return (moved, values - 8 * moved)

    move_x, inner_x = split_axis(coord_x)
    move_y, inner_y = split_axis(coord_y)
    move_z, inner_z = split_axis(coord_z)
    direction = 9 * (move_x + 1) + 3 * (move_y + 1) + (move_z + 1)
    inner = 64 * inner_x + 8 * inner_y + inner_z
    return (direction.astype(np.int32), inner.astype(np.int32))


def margin_tables():
    spots = np.arange(1000)
    return reach_tables(spots // 100 - 1, spots // 10 % 10 - 1, spots % 10 - 1)


def window_table():
    cells = np.arange(512)
    base = cells // 64 * 100 + cells // 8 % 8 * 10 + cells % 8
    shifts = np.arange(27)
    step = shifts // 9 * 100 + shifts // 3 % 3 * 10 + shifts % 3
    return (step[:, None] + base[None, :]).astype(np.int32)


def source_index(neighbors, direction, inner, spare):
    slots = jnp.take(neighbors, jnp.asarray(direction), axis=1)
    slots = jnp.where(slots < 0, spare, slots)
    return slots * 512 + jnp.asarray(inner)[None]


def pool_blocks(features, cell_ids, block_count):
    row_total = features.shape[1]
    step_rows = min(row_total, 2048)
    turns = row_total // step_rows
    targets = jnp.arange(block_count * 512, dtype=jnp.int32)
    width_here = features.shape[0]

    def accumulate(turn, carry):
        summed, tallies = carry
        rows = lax.dynamic_slice_in_dim(features, turn * step_rows, step_rows, 1)
        ids = lax.dynamic_slice_in_dim(cell_ids, turn * step_rows, step_rows, 0)
        onehot = (ids[:, None] == targets[None, :]).astype(jnp.bfloat16)
        summed = summed + jnp.dot(rows, onehot, preferred_element_type=jnp.float32)
        tallies = tallies + jnp.sum(onehot, axis=0, dtype=jnp.float32)
        return (summed, tallies)

    start = (
        jnp.zeros((width_here, block_count * 512), jnp.float32),
        jnp.zeros((block_count * 512,), jnp.float32),
    )
    summed, tallies = lax.fori_loop(0, turns, accumulate, start)
    voxels = (summed / jnp.maximum(tallies, 1.0)[None, :]).astype(jnp.bfloat16)
    return (voxels.reshape(width_here, block_count, 512), tallies)


def on_device(points, point_cell, conv_weight, conv_bias, neighbors):
    width_local = points.shape[0]
    owners = lax.axis_size("space")
    slot_total = points.shape[2]
    slot_cap = slot_total // owners
    block_count = neighbors.shape[0]
    arrived = lax.all_to_all(points, "space", split_axis=2, concat_axis=1, tiled=True)
    features = arrived.reshape(width_local, owners * slot_cap)
    cell_ids = point_cell[0]
    voxels, tallies = pool_blocks(features, cell_ids, block_count)
    active = jnp.where(tallies > 0.0, 1.0, 0.0).astype(jnp.float32)
    source = extended_2(voxels, (("space", 1),), block_count)
    source = jnp.concatenate([source, jnp.zeros((width_local, 1, 512), jnp.bfloat16)], 1)
    flat_source = source.reshape(width_local, (3 * block_count + 1) * 512)
    spare = 3 * block_count
    weight_all, bias_all = (
        lax.all_gather(conv_weight, "chan", axis=1, tiled=True),
        lax.all_gather(conv_bias, "chan", axis=0, tiled=True),
    )
    groups = lax.axis_size("chan")
    share = block_count // groups
    margin_dir, margin_inner = margin_tables()
    margin_index = source_index(neighbors, margin_dir, margin_inner, spare).reshape(
        block_count * 1000
    )
    margins = jnp.take(flat_source, margin_index, axis=1).reshape(width_local, block_count, 1000)
    spread = lax.all_to_all(margins, "chan", split_axis=1, concat_axis=0, tiled=True)
    width_all = spread.shape[0]
    flat_spread = spread.reshape(width_all, share * 1000)
    window = jnp.asarray(window_table())
    block_base = (jnp.arange(share, dtype=jnp.int32) * 1000)[None, :, None]
    column_index = (block_base + window[:, None, :]).reshape(27, share * 512)
    stacked = jnp.take(flat_spread, column_index, axis=1)
    total = jnp.zeros((width_all, share * 512), jnp.float32)
    for group in range(groups):
        low = group * width_local
        partial_sum = jnp.einsum(
            "ion,oic->cn",
            stacked[low : low + width_local],
            weight_all[:, low : low + width_local, :],
            preferred_element_type=jnp.float32,
        ).astype(jnp.bfloat16)
        partial_sum = lax.optimization_barrier(partial_sum)
        total = total + partial_sum.astype(jnp.float32)
    mine = lax.dynamic_slice_in_dim(active, lax.axis_index("chan") * (share * 512), share * 512, 0)
    finished = (
        jnp.maximum(total + bias_all.astype(jnp.float32)[:, None], 0.0) * mine[None, :]
    ).astype(jnp.bfloat16)
    voxel_out = lax.all_to_all(finished, "chan", split_axis=0, concat_axis=1, tiled=True)
    extended = jnp.concatenate([voxel_out, jnp.zeros((width_local, 1), jnp.bfloat16)], 1)
    picked = jnp.take(extended, cell_ids, axis=1).reshape(width_local, owners, slot_cap)
    returned = lax.all_to_all(picked, "space", split_axis=1, concat_axis=2, tiled=True)
    point_out = (points.astype(jnp.float32) + returned.astype(jnp.float32)).astype(jnp.bfloat16)
    return (voxel_out, point_out)


def solution(mesh):
    return jax.shard_map(
        on_device,
        mesh=mesh,
        in_specs=(
            P("chan", "space", None),
            P("space", None),
            P(None, "chan", None),
            P("chan"),
            P("space", None),
        ),
        out_specs=(P("chan", "space"), P("chan", "space", None)),
        check_vma=False,
    )
```

profile of v0, /device:TPU:0, one launch (start us, length us, event | category | flops | bytes accessed | tf_op | source)
XLA Modules:
  0.0 661.8 jit_solution(425877067838428987)
XLA Ops:
  7.2 17.2 %copy.80 = bf16[64,1,16384]{0,1,2:T(2,128)(2,1)} copy(bf16[64,1,16384]{2,0,1:T(8,128)(2,1)} %param.10) | data formatting | bytes 4194304 | tf_op args[0]
  24.9 90.8 %reduce.6 = bf16[16384,64]{1,0:T(8,128)(2,1)} reduce(bf16[16384,1,64]{2,1,0:T(2,128)(2,1)} %bitcast.73, bf16[]{:T(256)} %broadcast.224), dimensions={1}, to_apply=%bitcast.69.reduce_sub_computation | reduce | bytes 4194306
  115.6 7.6 %reshape.286 = bf16[8,2,65536]{2,1,0:T(2,128)(2,1)} reshape(bf16[16384,64]{1,0:T(8,128)(2,1)} %reduce.6) | data formatting | bytes 4194304
  123.2 5.3 all-to-all-start
  132.9 22.3 %all-to-all-done = bf16[8,2,65536]{2,1,0:T(2,128)(2,1)S(1)} async-done(((bf16[8,2,65536]{2,1,0:T(2,128)(2,1)}), bf16[8,2,65536]{2,1,0:T(2,128)(2,1)S(1)}, u32[]{:S(2)}, u32[]{:S(2)}) %all-to-all-start) | async-done | bytes 2097184 | tf_op jit(solution)/shard_map/all_to_all | solution.py:89
  155.2 5.9 reshape.287
  161.0 15.5 %copy.81 = bf16[64,1,16384]{2,0,1:T(8,128)(2,1)S(1)} copy(bf16[64,1,16384]{0,1,2:T(2,128)(2,1)} %bitcast.74) | data formatting | bytes 4194304 | tf_op jit(solution)/shard_map/all_to_all | solution.py:89
  176.6 115.7 %while.16 = (s32[]{:T(128)}, f32[64,4096]{1,0:T(8,128)}, f32[4096]{0:T(1024)S(1)}, bf16[64,16384]{1,0:T(8,128)(2,1)S(1)}, s32[16384]{0:T(1024)S(1)}, /*index=5*/s32[]{:T(128)}, s32[]{:T(128)}, s32[]{:T(128)}, s32[]{:T(128)}) while((s32[]{:T(128)}, f32[64,4096]{1,0:T(8,128)}, f32[4096]{0:T(1024)S(1)}, ...), condition=%wide.region_2.0_spmd.clone, body=%wide.region_0.0_spmd.clone.sunk | while | flops 1116213248 | bytes 2457758 | solution.py:78
  176.8 8.0 %fusion.65 = f32[64,4096]{1,0:T(8,128)} fusion(s32[2048]{0:T(1024)S(1)} %dynamic_slice.29, f32[64,4096]{1,0:T(8,128)} %get-tuple-element.202, pred[]{:T(512)S(6)} %compare.4, bf16[64,16384]{1,0:T(8,128)(2,1)S(1)} %get-tuple-element.213, s32[]{:T(128)S(6)} %select_n.172), kind=kOutput, calls=%fused_computation.10.clone.1 | convolution fusion | flops 1082654720 | bytes 2367493 | tf_op jit(solution)/shard_map/while/body/eval_jaxpr/dot_general | solution.py:70
  184.8 5.3 convert_reduce_fusion.2
  190.1 9.2 %fusion.65 = f32[64,4096]{1,0:T(8,128)} fusion(s32[2048]{0:T(1024)S(1)} %dynamic_slice.29, f32[64,4096]{1,0:T(8,128)} %get-tuple-element.202, pred[]{:T(512)S(6)} %compare.4, bf16[64,16384]{1,0:T(8,128)(2,1)S(1)} %get-tuple-element.213, s32[]{:T(128)S(6)} %select_n.172), kind=kOutput, calls=%fused_computation.10.clone.1 | convolution fusion | flops 1082654720 | bytes 2367493 | tf_op jit(solution)/shard_map/while/body/eval_jaxpr/dot_general | solution.py:70
  199.4 5.3 convert_reduce_fusion.2
  204.7 9.2 %fusion.65 = f32[64,4096]{1,0:T(8,128)} fusion(s32[2048]{0:T(1024)S(1)} %dynamic_slice.29, f32[64,4096]{1,0:T(8,128)} %get-tuple-element.202, pred[]{:T(512)S(6)} %compare.4, bf16[64,16384]{1,0:T(8,128)(2,1)S(1)} %get-tuple-element.213, s32[]{:T(128)S(6)} %select_n.172), kind=kOutput, calls=%fused_computation.10.clone.1 | convolution fusion | flops 1082654720 | bytes 2367493 | tf_op jit(solution)/shard_map/while/body/eval_jaxpr/dot_general | solution.py:70
  213.9 5.3 convert_reduce_fusion.2
  219.3 9.2 %fusion.65 = f32[64,4096]{1,0:T(8,128)} fusion(s32[2048]{0:T(1024)S(1)} %dynamic_slice.29, f32[64,4096]{1,0:T(8,128)} %get-tuple-element.202, pred[]{:T(512)S(6)} %compare.4, bf16[64,16384]{1,0:T(8,128)(2,1)S(1)} %get-tuple-element.213, s32[]{:T(128)S(6)} %select_n.172), kind=kOutput, calls=%fused_computation.10.clone.1 | convolution fusion | flops 1082654720 | bytes 2367493 | tf_op jit(solution)/shard_map/while/body/eval_jaxpr/dot_general | solution.py:70
  233.8 9.2 %fusion.65 = f32[64,4096]{1,0:T(8,128)} fusion(s32[2048]{0:T(1024)S(1)} %dynamic_slice.29, f32[64,4096]{1,0:T(8,128)} %get-tuple-element.202, pred[]{:T(512)S(6)} %compare.4, bf16[64,16384]{1,0:T(8,128)(2,1)S(1)} %get-tuple-element.213, s32[]{:T(128)S(6)} %select_n.172), kind=kOutput, calls=%fused_computation.10.clone.1 | convolution fusion | flops 1082654720 | bytes 2367493 | tf_op jit(solution)/shard_map/while/body/eval_jaxpr/dot_general | solution.py:70
  243.1 5.3 convert_reduce_fusion.2
  248.4 9.2 %fusion.65 = f32[64,4096]{1,0:T(8,128)} fusion(s32[2048]{0:T(1024)S(1)} %dynamic_slice.29, f32[64,4096]{1,0:T(8,128)} %get-tuple-element.202, pred[]{:T(512)S(6)} %compare.4, bf16[64,16384]{1,0:T(8,128)(2,1)S(1)} %get-tuple-element.213, s32[]{:T(128)S(6)} %select_n.172), kind=kOutput, calls=%fused_computation.10.clone.1 | convolution fusion | flops 1082654720 | bytes 2367493 | tf_op jit(solution)/shard_map/while/body/eval_jaxpr/dot_general | solution.py:70
  263.0 9.2 %fusion.65 = f32[64,4096]{1,0:T(8,128)} fusion(s32[2048]{0:T(1024)S(1)} %dynamic_slice.29, f32[64,4096]{1,0:T(8,128)} %get-tuple-element.202, pred[]{:T(512)S(6)} %compare.4, bf16[64,16384]{1,0:T(8,128)(2,1)S(1)} %get-tuple-element.213, s32[]{:T(128)S(6)} %select_n.172), kind=kOutput, calls=%fused_computation.10.clone.1 | convolution fusion | flops 1082654720 | bytes 2367493 | tf_op jit(solution)/shard_map/while/body/eval_jaxpr/dot_general | solution.py:70
  272.2 5.3 convert_reduce_fusion.2
  277.5 9.2 %fusion.65 = f32[64,4096]{1,0:T(8,128)} fusion(s32[2048]{0:T(1024)S(1)} %dynamic_slice.29, f32[64,4096]{1,0:T(8,128)} %get-tuple-element.202, pred[]{:T(512)S(6)} %compare.4, bf16[64,16384]{1,0:T(8,128)(2,1)S(1)} %get-tuple-element.213, s32[]{:T(128)S(6)} %select_n.172), kind=kOutput, calls=%fused_computation.10.clone.1 | convolution fusion | flops 1082654720 | bytes 2367493 | tf_op jit(solution)/shard_map/while/body/eval_jaxpr/dot_general | solution.py:70
  305.6 17.3 %gather_fusion.1 = bf16[8000,64]{1,0:T(8,128)(2,1)} fusion(bf16[64,12800]{0,1:T(8,128)(2,1)S(1)} %bitcast.72, s32[8192]{0:T(1024)S(1)} %pad_clamp_fusion), kind=kCustom, calls=%fused_computation.1 | custom fusion | bytes 2080000 | tf_op jit(solution)/shard_map/jit(_take)/gather | solution.py:108
  332.8 13.9 %all-reduce.1 = bf16[256]{0:T(256)(128)(2,1)S(1)} all-reduce(bf16[256]{0:T(256)(128)(2,1)S(1)} %dynamic-update-slice), channel_id=1, replica_groups=mesh['space'=8,'chan'=4] {'chan'}, use_global_device_ids=true, to_apply=%add.1 | all-reduce | flops 256 | bytes 1024
  348.1 6.2 all-to-all-done.1
  360.4 109.4 %gather_fusion.2 = bf16[27648,256]{1,0:T(8,128)(2,1)} fusion(bf16[256,2000]{0,1:T(8,128)(2,1)S(1)} %reshape.274, s32[27648]{0:T(1024)S(1)} %broadcast_clamp_fusion), kind=kCustom, calls=%fused_computation.2 | custom fusion | bytes 28422144 | tf_op jit(solution)/shard_map/jit(_take)/gather | solution.py:115
  469.8 18.7 %copy.88 = bf16[27,1024,256]{1,2,0:T(8,128)(2,1)} copy(bf16[27,1024,256]{2,1,0:T(8,128)(2,1)} %bitcast.71) | data formatting | bytes 28311552 | tf_op jit(solution)/shard_map/jit(_take)/gather | solution.py:115
  488.4 12.6 %select_bitcast_fusion = bf16[256,27,1024]{2,0,1:T(8,128)(2,1)} fusion(bf16[27,1024,256]{1,2,0:T(8,128)(2,1)} %copy.88, pred[27,1024]{1,0:T(8,128)(4,1)S(1)} %compare_and_fusion.1), kind=kLoop, calls=%fused_computation.14 | loop fusion | flops 7077888 | bytes 28339200 | tf_op jit(solution)/shard_map/jit(_take)/select_n | solution.py:115
  513.7 7.4 %all-to-all-start.2 = ((bf16[4,64,1024]{2,1,0:T(8,128)(2,1)}), bf16[4,64,1024]{2,1,0:T(8,128)(2,1)S(1)}, u32[]{:S(2)}, u32[]{:S(2)}) async-start(bf16[4,64,1024]{2,1,0:T(8,128)(2,1)} %bitcast.19), calls=%async_computation.2 | async-start | bytes 1048576 | tf_op jit(solution)/shard_map/all_to_all | solution.py:131
  521.1 15.1 %all-to-all-done.2 = bf16[4,64,1024]{2,1,0:T(8,128)(2,1)S(1)} async-done(((bf16[4,64,1024]{2,1,0:T(8,128)(2,1)}), bf16[4,64,1024]{2,1,0:T(8,128)(2,1)S(1)}, u32[]{:S(2)}, u32[]{:S(2)}) %all-to-all-start.2) | async-done | bytes 524320 | tf_op jit(solution)/shard_map/all_to_all | solution.py:131
  537.0 57.8 %gather_fusion.3 = bf16[16384,64]{1,0:T(8,128)(2,1)} fusion(bf16[64,4097]{0,1:T(8,128)(2,1)S(1)} %concatenate.7, s32[16384]{0:T(1024)S(1)} %broadcast_clamp_fusion.1), kind=kCustom, calls=%fused_computation.3 | custom fusion | bytes 4259840 | tf_op jit(solution)/shard_map/jit(_take)/gather | solution.py:133
  602.6 11.8 %all-to-all-start.3 = ((bf16[64,8,2048]{2,0,1:T(8,128)(2,1)}), bf16[64,8,2048]{2,0,1:T(8,128)(2,1)}, u32[]{:S(2)}, u32[]{:S(2)}) async-start(bf16[64,8,2048]{2,0,1:T(8,128)(2,1)} %broadcast_select_fusion), calls=%async_computation.3 | async-start | bytes 4194304 | tf_op jit(solution)/shard_map/all_to_all | solution.py:134
  615.6 25.6 %all-to-all-done.3 = bf16[64,8,2048]{2,0,1:T(8,128)(2,1)} async-done(((bf16[64,8,2048]{2,0,1:T(8,128)(2,1)}), bf16[64,8,2048]{2,0,1:T(8,128)(2,1)}, u32[]{:S(2)}, u32[]{:S(2)}) %all-to-all-start.3) | async-done | bytes 2097184 | tf_op jit(solution)/shard_map/all_to_all | solution.py:134
  (109 shorter events, 86.7 us)
Async XLA Ops:
  123.2 6.1 copy-start.6
  123.2 6.2 copy-start.7
  123.2 9.4 %copy-start.5 = (s32[1000]{0:T(1024)S(1)}, s32[1000]{0:T(1024)}, u32[]{:S(2)}) copy-start(s32[1000]{0:T(1024)} %constant.126.clone) | copy-start | bytes 12004
  123.2 9.5 %copy-start.3 = (s32[1,16384]{1,0:T(1,128)S(1)}, s32[1,16384]{1,0:T(1,128)}, u32[]{:S(2)}) copy-start(s32[1,16384]{1,0:T(1,128)} %param.11) | copy-start | bytes 196612
  123.2 32.0 %all-to-all-start = ((bf16[8,2,65536]{2,1,0:T(2,128)(2,1)}), bf16[8,2,65536]{2,1,0:T(2,128)(2,1)S(1)}, u32[]{:S(2)}, u32[]{:S(2)}) async-start(bf16[8,2,65536]{2,1,0:T(2,128)(2,1)} %reshape.286), calls=%async_computation | async-start | bytes 4194304 | tf_op jit(solution)/shard_map/all_to_all | solution.py:89
  128.6 372.5 %all-gather.2.cloned.1.call-start = ((), (), s32[]{:S(2)}) async-start(), calls=%async_computation.4 | async-start | bytes 4423680 | tf_op jit(solution)/shard_map/all_gather | solution.py:99
  293.8 3.3 collective-permute-start
  295.1 4.5 collective-permute-start.1
  322.9 8.0 %copy-start.4 = (s32[27,512]{1,0:T(8,128)S(1)}, s32[27,512]{1,0:T(8,128)}, u32[]{:S(2)}) copy-start(s32[27,512]{1,0:T(8,128)} %constant.127.clone) | copy-start | bytes 165892
  324.9 6.4 copy-start.10
  324.9 7.6 %copy-start.9 = (bf16[64]{0:T(256)(128)(2,1)S(1)}, bf16[64]{0:T(256)(128)(2,1)}, u32[]{:S(2)}) copy-start(bf16[64]{0:T(256)(128)(2,1)} %param.13) | copy-start | bytes 388
  326.0 28.3 %all-to-all-start.1 = ((bf16[64,8,1000]{2,0,1:T(8,128)(2,1)}), bf16[64,8,1000]{2,0,1:T(8,128)(2,1)S(1)}, u32[]{:S(2)}, u32[]{:S(2)}) async-start(bf16[64,8,1000]{2,0,1:T(8,128)(2,1)} %broadcast_select_fusion.1), calls=%async_computation.1 | async-start | bytes 2097152 | tf_op jit(solution)/shard_map/all_to_all | solution.py:109
  354.3 1.0 copy-start.2
  501.0 6.4 copy-start
  507.4 2.5 copy-start.8
  513.7 22.6 %all-to-all-start.2 = ((bf16[4,64,1024]{2,1,0:T(8,128)(2,1)}), bf16[4,64,1024]{2,1,0:T(8,128)(2,1)S(1)}, u32[]{:S(2)}, u32[]{:S(2)}) async-start(bf16[4,64,1024]{2,1,0:T(8,128)(2,1)} %bitcast.19), calls=%async_computation.2 | async-start | bytes 1048576 | tf_op jit(solution)/shard_map/all_to_all | solution.py:131
  602.6 38.6 %all-to-all-start.3 = ((bf16[64,8,2048]{2,0,1:T(8,128)(2,1)}), bf16[64,8,2048]{2,0,1:T(8,128)(2,1)}, u32[]{:S(2)}, u32[]{:S(2)}) async-start(bf16[64,8,2048]{2,0,1:T(8,128)(2,1)} %broadcast_select_fusion), calls=%async_computation.3 | async-start | bytes 4194304 | tf_op jit(solution)/shard_map/all_to_all | solution.py:134
  646.0 5.1 copy-start.1
Sparse Core Ops, SparseCore 0:
  130.9 71.6 all-gather.1
where the time goes:
time: 665 us; the launch traced here: 662 us
  local copies, waits for them, and re-layouts  288 us (43%)
  other arithmetic  159 us (24%)
  matrix products  81 us (12%)
  waiting for transfers between devices  72.4 us (11%)
  starting transfers between devices  32.1 us (5%)
  between operations  15.1 us (2%)
  blocking collectives  13.9 us (2%)
    gather x2, local copies, waits for them, and re-layouts, on_device(): stacked = jnp.take(flat_spread, column_index, axis=1)  128 us
    unnamed x4, other arithmetic  91.6 us
    dot_general x8, matrix products, accumulate(): summed = summed + jnp.dot(rows, onehot, preferred_element_type=jnp.float32)  72.6 us
    gather x2, local copies, waits for them, and re-layouts, on_device(): jnp.take(extended, cell_ids, axis=1).reshape(width_local, owners, slot_cap)  62.5 us
    reduce_sum x8, other arithmetic, accumulate(): tallies = tallies + jnp.sum(onehot, axis=0, dtype=jnp.float32)  42.2 us
    unnamed x37, local copies, waits for them, and re-layouts  37.8 us
    all_to_all x1, waiting for transfers between devices, on_device(): lax.all_to_all(picked, 'space', split_axis=1, concat_axis=2, tiled=True)  25.6 us
    all_to_all x1, waiting for transfers between devices, on_device(): lax.all_to_all(points, 'space', split_axis=2, concat_axis=1, tiled=True)  22.3 us
  transfers between devices with their start and end apart: 7, of which 5 were waited for; matrix products, arithmetic and copies ran while one was open for 48% of the time, Pallas kernels for 0%

commit v1 on v0

--- a/solution.py
+++ b/solution.py
@@ -86,7 +86,10 @@
     slot_total = points.shape[2]
     slot_cap = slot_total // owners
     block_count = neighbors.shape[0]
-    arrived = lax.all_to_all(points, "space", split_axis=2, concat_axis=1, tiled=True)
+    arrived = jnp.concatenate(
+        lax.all_to_all(jnp.stack(jnp.split(points, lax.axis_size("space"), axis=2)), "space", 0, 0),
+        axis=1,
+    )
     features = arrived.reshape(width_local, owners * slot_cap)
     cell_ids = point_cell[0]
     voxels, tallies = pool_blocks(features, cell_ids, block_count)

time: 665 us -> 540 us (0.81)
  other arithmetic: 159 us -> 68.2 us
  local copies, waits for them, and re-layouts: 288 us -> 255 us
    unnamed x4 -> x3, other arithmetic: 91.6 us -> 0.8 us
    unnamed x37 -> x41, local copies, waits for them, and re-layouts: 37.8 us -> 19.9 us
    all_to_all x1 -> x0, local copies, waits for them, and re-layouts: 15.5 us -> none  [on_device(): lax.all_to_all(points, 'space', split_axis=2, concat_axis=1, tiled=True)]
  transfers between devices with their start and end apart: 7 -> 7, of which waited for: 5 -> 5; matrix products, arithmetic and copies ran while one was open for 48% -> 55% of each run, Pallas kernels for 0% -> 0%
where the time goes in v1:
time: 540 us; the launch traced here: 539 us
  local copies, waits for them, and re-layouts  255 us (47%)
  matrix products  81.9 us (15%)
  waiting for transfers between devices  72.4 us (13%)
  other arithmetic  68.2 us (13%)
  starting transfers between devices  31.8 us (6%)
  between operations  15.1 us (3%)
  blocking collectives  13.9 us (3%)
    gather x2, local copies, waits for them, and re-layouts, on_device(): stacked = jnp.take(flat_spread, column_index, axis=1)  127 us
    dot_general x8, matrix products, accumulate(): summed = summed + jnp.dot(rows, onehot, preferred_element_type=jnp.float32)  73.4 us
    gather x2, local copies, waits for them, and re-layouts, on_device(): jnp.take(extended, cell_ids, axis=1).reshape(width_local, owners, slot_cap)  62.2 us
    reduce_sum x8, other arithmetic, accumulate(): tallies = tallies + jnp.sum(onehot, axis=0, dtype=jnp.float32)  42.3 us
    all_to_all x1, waiting for transfers between devices, on_device(): lax.all_to_all(picked, 'space', split_axis=1, concat_axis=2, tiled=True)  25.6 us
    all_to_all x1, waiting for transfers between devices, on_device(): lax.all_to_all(jnp.stack(jnp.split(points, lax.axis_size('space'), axis=2...  22.3 us
    unnamed x41, local copies, waits for them, and re-layouts  19.9 us
    gather x2, local copies, waits for them, and re-layouts, on_device(): jnp.take(flat_source, margin_index, axis=1)  19.2 us
  transfers between devices with their start and end apart: 7, of which 5 were waited for; matrix products, arithmetic and copies ran while one was open for 55% of the time, Pallas kernels for 0%

profile of v1, /device:TPU:0, one launch (start us, length us, event | category | flops | bytes accessed | tf_op | source)
XLA Modules:
  0.0 538.7 jit_solution(11126708305411356537)
XLA Ops:
  20.6 5.2 all-to-all-start
  30.1 22.3 %all-to-all-done = bf16[8,64,1,2048]{3,1,2,0:T(8,128)(2,1)S(1)} async-done(((bf16[8,64,1,2048]{3,1,2,0:T(8,128)(2,1)}), bf16[8,64,1,2048]{3,1,2,0:T(8,128)(2,1)S(1)}, u32[]{:S(2)}, u32[]{:S(2)}) %all-to-all-start) | async-done | bytes 2097184 | tf_op jit(solution)/shard_map/all_to_all | solution.py:90
  53.9 116.3 %while.16 = (s32[]{:T(128)}, f32[64,4096]{1,0:T(8,128)}, f32[4096]{0:T(1024)S(1)}, bf16[64,16384]{1,0:T(8,128)(2,1)}, s32[16384]{0:T(1024)S(1)}, /*index=5*/s32[]{:T(128)}, s32[]{:T(128)}, s32[]{:T(128)}, s32[]{:T(128)}) while((s32[]{:T(128)}, f32[64,4096]{1,0:T(8,128)}, f32[4096]{0:T(1024)S(1)}, bf16[64,16384]{1,0:T(8,128)(2,1)}, ...), condition=%wide.region_2.0_spmd.clone, body=%wide.region_0.0_spmd.clone.sunk | while | flops 1116213248 | bytes 2457758 | solution.py:78
  53.9 8.9 %fusion.65 = f32[64,4096]{1,0:T(8,128)} fusion(s32[2048]{0:T(1024)S(1)} %dynamic_slice.29, f32[64,4096]{1,0:T(8,128)} %get-tuple-element.197, pred[]{:T(512)S(6)} %compare.4, bf16[64,16384]{1,0:T(8,128)(2,1)} %get-tuple-element.208, s32[]{:T(128)S(6)} %select_n.172), kind=kOutput, calls=%fused_computation.10.clone.1 | convolution fusion | flops 1082654720 | bytes 2367493 | tf_op jit(solution)/shard_map/while/body/eval_jaxpr/dot_general | solution.py:70
  62.7 5.3 convert_reduce_fusion.2
  68.1 9.2 %fusion.65 = f32[64,4096]{1,0:T(8,128)} fusion(s32[2048]{0:T(1024)S(1)} %dynamic_slice.29, f32[64,4096]{1,0:T(8,128)} %get-tuple-element.197, pred[]{:T(512)S(6)} %compare.4, bf16[64,16384]{1,0:T(8,128)(2,1)} %get-tuple-element.208, s32[]{:T(128)S(6)} %select_n.172), kind=kOutput, calls=%fused_computation.10.clone.1 | convolution fusion | flops 1082654720 | bytes 2367493 | tf_op jit(solution)/shard_map/while/body/eval_jaxpr/dot_general | solution.py:70
  77.3 5.3 convert_reduce_fusion.2
  82.6 9.2 %fusion.65 = f32[64,4096]{1,0:T(8,128)} fusion(s32[2048]{0:T(1024)S(1)} %dynamic_slice.29, f32[64,4096]{1,0:T(8,128)} %get-tuple-element.197, pred[]{:T(512)S(6)} %compare.4, bf16[64,16384]{1,0:T(8,128)(2,1)} %get-tuple-element.208, s32[]{:T(128)S(6)} %select_n.172), kind=kOutput, calls=%fused_computation.10.clone.1 | convolution fusion | flops 1082654720 | bytes 2367493 | tf_op jit(solution)/shard_map/while/body/eval_jaxpr/dot_general | solution.py:70
  91.9 5.3 convert_reduce_fusion.2
  97.2 9.2 %fusion.65 = f32[64,4096]{1,0:T(8,128)} fusion(s32[2048]{0:T(1024)S(1)} %dynamic_slice.29, f32[64,4096]{1,0:T(8,128)} %get-tuple-element.197, pred[]{:T(512)S(6)} %compare.4, bf16[64,16384]{1,0:T(8,128)(2,1)} %get-tuple-element.208, s32[]{:T(128)S(6)} %select_n.172), kind=kOutput, calls=%fused_computation.10.clone.1 | convolution fusion | flops 1082654720 | bytes 2367493 | tf_op jit(solution)/shard_map/while/body/eval_jaxpr/dot_general | solution.py:70
  106.4 5.3 convert_reduce_fusion.2
  111.8 9.2 %fusion.65 = f32[64,4096]{1,0:T(8,128)} fusion(s32[2048]{0:T(1024)S(1)} %dynamic_slice.29, f32[64,4096]{1,0:T(8,128)} %get-tuple-element.197, pred[]{:T(512)S(6)} %compare.4, bf16[64,16384]{1,0:T(8,128)(2,1)} %get-tuple-element.208, s32[]{:T(128)S(6)} %select_n.172), kind=kOutput, calls=%fused_computation.10.clone.1 | convolution fusion | flops 1082654720 | bytes 2367493 | tf_op jit(solution)/shard_map/while/body/eval_jaxpr/dot_general | solution.py:70
  121.0 5.3 convert_reduce_fusion.2
  126.3 9.2 %fusion.65 = f32[64,4096]{1,0:T(8,128)} fusion(s32[2048]{0:T(1024)S(1)} %dynamic_slice.29, f32[64,4096]{1,0:T(8,128)} %get-tuple-element.197, pred[]{:T(512)S(6)} %compare.4, bf16[64,16384]{1,0:T(8,128)(2,1)} %get-tuple-element.208, s32[]{:T(128)S(6)} %select_n.172), kind=kOutput, calls=%fused_computation.10.clone.1 | convolution fusion | flops 1082654720 | bytes 2367493 | tf_op jit(solution)/shard_map/while/body/eval_jaxpr/dot_general | solution.py:70
  135.5 5.3 convert_reduce_fusion.2
  140.9 9.2 %fusion.65 = f32[64,4096]{1,0:T(8,128)} fusion(s32[2048]{0:T(1024)S(1)} %dynamic_slice.29, f32[64,4096]{1,0:T(8,128)} %get-tuple-element.197, pred[]{:T(512)S(6)} %compare.4, bf16[64,16384]{1,0:T(8,128)(2,1)} %get-tuple-element.208, s32[]{:T(128)S(6)} %select_n.172), kind=kOutput, calls=%fused_computation.10.clone.1 | convolution fusion | flops 1082654720 | bytes 2367493 | tf_op jit(solution)/shard_map/while/body/eval_jaxpr/dot_general | solution.py:70
  150.1 5.3 convert_reduce_fusion.2
  155.4 9.2 %fusion.65 = f32[64,4096]{1,0:T(8,128)} fusion(s32[2048]{0:T(1024)S(1)} %dynamic_slice.29, f32[64,4096]{1,0:T(8,128)} %get-tuple-element.197, pred[]{:T(512)S(6)} %compare.4, bf16[64,16384]{1,0:T(8,128)(2,1)} %get-tuple-element.208, s32[]{:T(128)S(6)} %select_n.172), kind=kOutput, calls=%fused_computation.10.clone.1 | convolution fusion | flops 1082654720 | bytes 2367493 | tf_op jit(solution)/shard_map/while/body/eval_jaxpr/dot_general | solution.py:70
  164.7 5.3 convert_reduce_fusion.2
  183.5 17.3 %gather_fusion.1 = bf16[8000,64]{1,0:T(8,128)(2,1)} fusion(bf16[64,12800]{0,1:T(8,128)(2,1)S(1)} %bitcast.92, s32[8192]{0:T(1024)S(1)} %pad_clamp_fusion), kind=kCustom, calls=%fused_computation.1 | custom fusion | bytes 2080000 | tf_op jit(solution)/shard_map/jit(_take)/gather | solution.py:111
  203.9 4.8 all-to-all-start.1
  210.6 13.9 %all-reduce.1 = bf16[256]{0:T(256)(128)(2,1)S(1)} all-reduce(bf16[256]{0:T(256)(128)(2,1)S(1)} %dynamic-update-slice), channel_id=1, replica_groups=mesh['space'=8,'chan'=4] {'chan'}, use_global_device_ids=true, to_apply=%add.1 | all-reduce | flops 256 | bytes 1024
  226.0 6.2 %all-to-all-done.1 = bf16[64,8,1000]{2,0,1:T(8,128)(2,1)S(1)} async-done(((bf16[64,8,1000]{2,0,1:T(8,128)(2,1)}), bf16[64,8,1000]{2,0,1:T(8,128)(2,1)S(1)}, u32[]{:S(2)}, u32[]{:S(2)}) %all-to-all-start.1) | async-done | bytes 1024032 | tf_op jit(solution)/shard_map/all_to_all | solution.py:112
  238.2 108.8 %gather_fusion.2 = bf16[27648,256]{1,0:T(8,128)(2,1)} fusion(bf16[256,2000]{0,1:T(8,128)(2,1)S(1)} %reshape.270, s32[27648]{0:T(1024)S(1)} %broadcast_clamp_fusion), kind=kCustom, calls=%fused_computation.2 | custom fusion | bytes 28422144 | tf_op jit(solution)/shard_map/jit(_take)/gather | solution.py:118
  347.1 18.6 %copy.88 = bf16[27,1024,256]{1,2,0:T(8,128)(2,1)} copy(bf16[27,1024,256]{2,1,0:T(8,128)(2,1)} %bitcast.91) | data formatting | bytes 28311552 | tf_op jit(solution)/shard_map/jit(_take)/gather | solution.py:118
  365.7 12.6 %select_bitcast_fusion = bf16[256,27,1024]{2,0,1:T(8,128)(2,1)} fusion(bf16[27,1024,256]{1,2,0:T(8,128)(2,1)} %copy.88, pred[27,1024]{1,0:T(8,128)(4,1)S(1)} %compare_and_fusion.1), kind=kLoop, calls=%fused_computation.14 | loop fusion | flops 7077888 | bytes 28339200 | tf_op jit(solution)/shard_map/jit(_take)/select_n | solution.py:118
  391.0 7.4 %all-to-all-start.2 = ((bf16[4,64,1024]{2,1,0:T(8,128)(2,1)}), bf16[4,64,1024]{2,1,0:T(8,128)(2,1)S(1)}, u32[]{:S(2)}, u32[]{:S(2)}) async-start(bf16[4,64,1024]{2,1,0:T(8,128)(2,1)} %bitcast.27), calls=%async_computation.2 | async-start | bytes 1048576 | tf_op jit(solution)/shard_map/all_to_all | solution.py:134
  398.4 15.2 %all-to-all-done.2 = bf16[4,64,1024]{2,1,0:T(8,128)(2,1)S(1)} async-done(((bf16[4,64,1024]{2,1,0:T(8,128)(2,1)}), bf16[4,64,1024]{2,1,0:T(8,128)(2,1)S(1)}, u32[]{:S(2)}, u32[]{:S(2)}) %all-to-all-start.2) | async-done | bytes 524320 | tf_op jit(solution)/shard_map/all_to_all | solution.py:134
  414.3 57.4 %gather_fusion.3 = bf16[16384,64]{1,0:T(8,128)(2,1)} fusion(bf16[64,4097]{0,1:T(8,128)(2,1)S(1)} %concatenate.7, s32[16384]{0:T(1024)S(1)} %broadcast_clamp_fusion.1), kind=kCustom, calls=%fused_computation.3 | custom fusion | bytes 4259840 | tf_op jit(solution)/shard_map/jit(_take)/gather | solution.py:136
  479.6 11.8 %all-to-all-start.3 = ((bf16[64,8,2048]{2,0,1:T(8,128)(2,1)}), bf16[64,8,2048]{2,0,1:T(8,128)(2,1)}, u32[]{:S(2)}, u32[]{:S(2)}) async-start(bf16[64,8,2048]{2,0,1:T(8,128)(2,1)} %broadcast_select_fusion), calls=%async_computation.3 | async-start | bytes 4194304 | tf_op jit(solution)/shard_map/all_to_all | solution.py:137
  492.5 25.6 %all-to-all-done.3 = bf16[64,8,2048]{2,0,1:T(8,128)(2,1)} async-done(((bf16[64,8,2048]{2,0,1:T(8,128)(2,1)}), bf16[64,8,2048]{2,0,1:T(8,128)(2,1)}, u32[]{:S(2)}, u32[]{:S(2)}) %all-to-all-start.3) | async-done | bytes 2097184 | tf_op jit(solution)/shard_map/all_to_all | solution.py:137
  522.8 5.1 reshape.227
  (112 shorter events, 75.2 us)
Async XLA Ops:
  15.5 11.0 %copy-start.6 = (s32[8,27]{1,0:T(8,128)S(1)}, s32[8,27]{1,0:T(8,128)}, u32[]{:S(2)}) copy-start(s32[8,27]{1,0:T(8,128)} %param.14) | copy-start | bytes 2596
  15.5 11.1 %copy-start.7 = (s32[1000]{0:T(1024)S(1)}, s32[1000]{0:T(1024)}, u32[]{:S(2)}) copy-start(s32[1000]{0:T(1024)} %constant.140) | copy-start | bytes 12004
  18.9 11.0 %copy-start.5 = (s32[1000]{0:T(1024)S(1)}, s32[1000]{0:T(1024)}, u32[]{:S(2)}) copy-start(s32[1000]{0:T(1024)} %constant.126.clone) | copy-start | bytes 12004
  18.9 11.1 %copy-start.3 = (s32[1,16384]{1,0:T(1,128)S(1)}, s32[1,16384]{1,0:T(1,128)}, u32[]{:S(2)}) copy-start(s32[1,16384]{1,0:T(1,128)} %param.11) | copy-start | bytes 196612
  20.6 31.8 %all-to-all-start = ((bf16[8,64,1,2048]{3,1,2,0:T(8,128)(2,1)}), bf16[8,64,1,2048]{3,1,2,0:T(8,128)(2,1)S(1)}, u32[]{:S(2)}, u32[]{:S(2)}) async-start(bf16[8,64,1,2048]{3,1,2,0:T(8,128)(2,1)} %bitcast_dynamic-update-slice_fusion), calls=%async_computation | async-start | bytes 4194304 | tf_op jit(solution)/shard_map/all_to_all | solution.py:90
  25.8 352.6 %all-gather.2.cloned.1.call-start = ((), (), s32[]{:S(2)}) async-start(), calls=%async_computation.4 | async-start | bytes 4423680 | tf_op jit(solution)/shard_map/all_gather | solution.py:102
  171.6 3.3 collective-permute-start
  173.0 4.5 collective-permute-start.1
  200.8 7.9 %copy-start.4 = (s32[27,512]{1,0:T(8,128)S(1)}, s32[27,512]{1,0:T(8,128)}, u32[]{:S(2)}) copy-start(s32[27,512]{1,0:T(8,128)} %constant.127.clone) | copy-start | bytes 165892
  202.8 6.3 %copy-start.10 = (u32[32]{0:T(128)S(1)}, u32[32]{0:T(128)}, u32[]{:S(2)}) copy-start(u32[32]{0:T(128)} %constant.143) | copy-start | bytes 388
  202.8 7.6 %copy-start.9 = (bf16[64]{0:T(256)(128)(2,1)S(1)}, bf16[64]{0:T(256)(128)(2,1)}, u32[]{:S(2)}) copy-start(bf16[64]{0:T(256)(128)(2,1)} %param.13) | copy-start | bytes 388
  203.9 28.3 %all-to-all-start.1 = ((bf16[64,8,1000]{2,0,1:T(8,128)(2,1)}), bf16[64,8,1000]{2,0,1:T(8,128)(2,1)S(1)}, u32[]{:S(2)}, u32[]{:S(2)}) async-start(bf16[64,8,1000]{2,0,1:T(8,128)(2,1)} %broadcast_select_fusion.1), calls=%async_computation.1 | async-start | bytes 2097152 | tf_op jit(solution)/shard_map/all_to_all | solution.py:112
  232.1 1.0 copy-start.2
  378.3 6.4 %copy-start = (bf16[256,27,1024]{2,0,1:T(8,128)(2,1)S(1)}, bf16[256,27,1024]{2,0,1:T(8,128)(2,1)}, u32[]{:S(2)}) copy-start(bf16[256,27,1024]{2,0,1:T(8,128)(2,1)} %select_bitcast_fusion) | copy-start | bytes 42467332
  384.7 2.5 copy-start.8
  391.0 22.6 %all-to-all-start.2 = ((bf16[4,64,1024]{2,1,0:T(8,128)(2,1)}), bf16[4,64,1024]{2,1,0:T(8,128)(2,1)S(1)}, u32[]{:S(2)}, u32[]{:S(2)}) async-start(bf16[4,64,1024]{2,1,0:T(8,128)(2,1)} %bitcast.27), calls=%async_computation.2 | async-start | bytes 1048576 | tf_op jit(solution)/shard_map/all_to_all | solution.py:134
  479.6 38.5 %all-to-all-start.3 = ((bf16[64,8,2048]{2,0,1:T(8,128)(2,1)}), bf16[64,8,2048]{2,0,1:T(8,128)(2,1)}, u32[]{:S(2)}, u32[]{:S(2)}) async-start(bf16[64,8,2048]{2,0,1:T(8,128)(2,1)} %broadcast_select_fusion), calls=%async_computation.3 | async-start | bytes 4194304 | tf_op jit(solution)/shard_map/all_to_all | solution.py:137
  522.8 5.1 copy-start.1
Sparse Core Ops, SparseCore 0:
  28.2 71.6 all-gather.1
